TPU v7x, 32 devices: a whole 2x2x4 slice. The times are simulated.
32 devices in a mesh: feat: 8 (over z, y), tok: 4 (over x, core).
Axes of the slice: x: 2, y: 2, z: 4, core: 2. Of those that a mesh axis runs over, the one named last changes fastest.
Arguments:
- tokens: bfloat16 [4096, 8192], P('tok', 'feat'), parts along dimension 0, may hold values from -6 to 6
- pair_weights: bfloat16 [2, 2048, 8192], P(None, None, 'feat'), may hold values from -0.125 to 0.125
- rank_down: bfloat16 [8192, 256], P('feat'), may hold values from -0.0625 to 0.0625
- rank_up: bfloat16 [256, 8192], P(None, 'feat'), may hold values from -0.375 to 0.375
Outputs:
- mixed: bfloat16 [4096, 8192], P('tok', 'feat'), parts along dimension 0
There are 4 independent parts, one for each index of `tok`. A program takes and returns all parts, laid end to end along the dimension named above; an argument that names none is the same for every part. Nothing has to cross between parts.
All inputs are finite; a program needn't handle non-finite values.
Results may differ from a plain program's by a relative error of at most 0.0049.
Values may be sent and summed in bfloat16 or wider, within the bound.
A program may use at most 64 MiB of HBM per device.

v0:
```python
import jax
import jax.numpy as jnp
from jax import lax
from jax.sharding import PartitionSpec as P


def swapped(block, axis, stride):
    count = lax.axis_size(axis)
    route = []
    for low in range(count):
        high = low | 1 << stride
        if high != low and high < count:
            route += [(low, high), (high, low)]
    return lax.ppermute(block, axis, route)


def pair_product(own_rows, partner_rows, section_weight):
    block_width = own_rows.shape[1]
    first = jnp.dot(own_rows, section_weight[:block_width], preferred_element_type=jnp.float32)
    second = jnp.dot(partner_rows, section_weight[block_width:], preferred_element_type=jnp.float32)
    return first + second


def on_device(tokens, pair_weights, rank_down, rank_up):
    bit_levels = lax.axis_size("feat").bit_length() - 1
    section_count = pair_weights.shape[0]
    current = tokens
    activated = None
    for section_index in range(section_count):
        bit_number = section_index * (bit_levels - 1) // (section_count - 1)
        section_weight = pair_weights[section_index]
        half_rows = current.shape[0] // 2
        half_parts = []
        for half_index in range(2):
            own_rows = current[half_index * half_rows : (half_index + 1) * half_rows]
            partner_rows = swapped(own_rows, "feat", bit_number)
            half_parts.append(pair_product(own_rows, partner_rows, section_weight))
        pre_act = jnp.concatenate(half_parts, 0)
        activated = jax.nn.silu(pre_act)
        current = activated.astype(jnp.bfloat16)
    partial_value = jnp.dot(tokens, rank_down, preferred_element_type=jnp.float32)
    rank_total = lax.psum(partial_value, "feat")
    branch_out = jnp.dot(
        rank_total.astype(jnp.bfloat16), rank_up, preferred_element_type=jnp.float32
    )
    return (activated + branch_out).astype(jnp.bfloat16)


def solution(mesh):
    return jax.shard_map(
        on_device,
        mesh=mesh,
        in_specs=(P("tok", "feat"), P(None, None, "feat"), P("feat", None), P(None, "feat")),
        out_specs=P("tok", "feat"),
        check_vma=False,
    )
```

profile of v0, /device:TPU:0, one launch (start us, length us, event | category | flops | bytes accessed | tf_op | source)
XLA Modules:
  0.0 207.6 jit_solution(4900862130040518110)
XLA Ops:
  0.0 0.0 copy-start
  0.0 0.0 copy-start.1
  0.0 0.0 copy-start.2
  0.0 1.9 fusion.42
  1.9 3.1 %collective-permute-start = (bf16[512,1024]{1,0:T(8,128)(2,1)S(1)}, bf16[512,1024]{1,0:T(8,128)(2,1)S(1)}, u32[]{:S(2)}, u32[]{:S(2)}) collective-permute-start(bf16[512,1024]{1,0:T(8,128)(2,1)S(1)} %get-tuple-element.7), channel_id=1, source_target_pairs={{0,4},{4,0},{8,12},{12,8},{16,20},{20,16},{24,28},{28,24},{1,5},{5... | collective-permute-start | bytes 3145736 | tf_op jit(solution)/shard_map/ppermute | solution.py:14
  4.9 0.1 collective-permute-start.1
  5.0 0.0 copy-done.1
  5.0 0.0 copy-done.2
  5.0 0.0 slice-start
  5.0 1.7 fusion.43
  6.7 0.0 slice-start.1
  6.7 3.0 %fusion.14 = f32[512,1024]{1,0:T(8,128)S(1)} fusion(bf16[2,2048,1024]{2,1,0:T(8,128)(2,1)} %param.5, bf16[1024,1024]{1,0:T(8,128)(2,1)S(1)} %copy-done.1), kind=kOutput, calls=%fused_computation.18 | convolution fusion | flops 1073741824 | bytes 5242880 | tf_op jit(solution)/shard_map/dot_general | solution.py:19
  9.7 0.0 slice-done
  9.8 0.0 slice-done.1
  9.8 1.3 fusion.12
  11.1 17.9 %collective-permute-done = bf16[512,1024]{1,0:T(8,128)(2,1)S(1)} collective-permute-done((bf16[512,1024]{1,0:T(8,128)(2,1)S(1)}, bf16[512,1024]{1,0:T(8,128)(2,1)S(1)}, u32[]{:S(2)}, u32[]{:S(2)}) %collective-permute-start) | collective-permute-done | bytes 1048608 | tf_op jit(solution)/shard_map/ppermute | solution.py:14
  29.0 1.3 fusion.24
  30.2 20.3 %collective-permute-done.1 = bf16[512,1024]{1,0:T(8,128)(2,1)S(1)} collective-permute-done((bf16[512,1024]{1,0:T(8,128)(2,1)S(1)}, bf16[512,1024]{1,0:T(8,128)(2,1)S(1)}, u32[]{:S(2)}, u32[]{:S(2)}) %collective-permute-start.1) | collective-permute-done | bytes 1048608 | tf_op jit(solution)/shard_map/ppermute | solution.py:14
  50.6 1.3 fusion.27
  51.9 1.2 multiply_convert_fusion
  53.0 1.5 fusion.41
  54.5 2.8 %collective-permute-start.2 = (bf16[512,1024]{1,0:T(8,128)(2,1)}, bf16[512,1024]{1,0:T(8,128)(2,1)}, u32[]{:S(2)}, u32[]{:S(2)}) collective-permute-start(bf16[512,1024]{1,0:T(8,128)(2,1)} %get-tuple-element.5), channel_id=1, source_target_pairs={{0,16},{16,0},{4,20},{20,4},{8,24},{24,8},{12,28},{28,12},{1,17},{... | collective-permute-start | bytes 3145736 | tf_op jit(solution)/shard_map/ppermute | solution.py:14
  57.3 110.3 %all-reduce.1 = bf16[1024,256]{1,0:T(8,128)(2,1)S(1)} all-reduce(f32[1024,256]{1,0:T(8,128)} %fusion.43), channel_id=1, replica_groups=mesh['feat'=8,'tok'=4] {'feat'}, use_global_device_ids=true, to_apply=%region_0.1 | all-reduce | flops 262144 | bytes 1572864 | tf_op jit(solution)/shard_map/psum | solution.py:42
  167.6 18.0 %collective-permute-start.3 = (bf16[512,1024]{1,0:T(8,128)(2,1)}, bf16[512,1024]{1,0:T(8,128)(2,1)S(1)}, u32[]{:S(2)}, u32[]{:S(2)}) collective-permute-start(bf16[512,1024]{1,0:T(8,128)(2,1)} %get-tuple-element.6), channel_id=1, source_target_pairs={{0,16},{16,0},{4,20},{20,4},{8,24},{24,8},{12,28},{28,12},{1,17},{... | collective-permute-start | bytes 3145736 | tf_op jit(solution)/shard_map/ppermute | solution.py:14
  185.6 0.0 slice-start.2
  185.6 3.0 %fusion.6 = f32[512,1024]{1,0:T(8,128)S(1)} fusion(bf16[2,2048,1024]{2,1,0:T(8,128)(2,1)} %param.5, bf16[1024,1024]{1,0:T(8,128)(2,1)S(1)} %multiply_convert_fusion), kind=kOutput, calls=%fused_computation.10 | convolution fusion | flops 1073741824 | bytes 5242880 | tf_op jit(solution)/shard_map/dot_general | solution.py:19
  188.6 0.0 slice-start.3
  188.6 3.0 %fusion.4 = f32[512,1024]{1,0:T(8,128)S(1)} fusion(bf16[2,2048,1024]{2,1,0:T(8,128)(2,1)} %param.5, bf16[1024,1024]{1,0:T(8,128)(2,1)S(1)} %multiply_convert_fusion), kind=kOutput, calls=%fused_computation.8 | convolution fusion | flops 1073741824 | bytes 5242880 | tf_op jit(solution)/shard_map/dot_general | solution.py:19
  191.6 0.0 collective-permute-done.2
  191.6 0.0 slice-done.2
  191.6 0.0 slice-done.3
  191.7 2.5 %fusion.30 = f32[512,1024]{1,0:T(8,128)S(1)} fusion(f32[512,1024]{1,0:T(8,128)S(1)} %fusion.6, bf16[512,1024]{1,0:T(8,128)(2,1)} %collective-permute-done.2, bf16[2,2048,1024]{2,1,0:T(8,128)(2,1)S(1)} %bitcast.39), kind=kOutput, calls=%fused_computation.30 | convolution fusion | flops 1074266112 | bytes 7340032 | tf_op jit(solution)/shard_map/dot_general | solution.py:20
  194.2 9.6 %collective-permute-done.3 = bf16[512,1024]{1,0:T(8,128)(2,1)S(1)} collective-permute-done((bf16[512,1024]{1,0:T(8,128)(2,1)}, bf16[512,1024]{1,0:T(8,128)(2,1)S(1)}, u32[]{:S(2)}, u32[]{:S(2)}) %collective-permute-start.3) | collective-permute-done | bytes 1048608 | tf_op jit(solution)/shard_map/ppermute | solution.py:14
  203.8 1.3 fusion.33
  205.0 0.0 copy-done
  205.1 2.6 %add_convert_fusion = bf16[1024,1024]{1,0:T(8,128)(2,1)} fusion(f32[512,1024]{1,0:T(8,128)S(1)} %fusion.33, f32[512,1024]{1,0:T(8,128)S(1)} %fusion.30, bf16[256,1024]{1,0:T(8,128)(2,1)S(1)} %copy-done, bf16[1024,256]{1,0:T(8,128)(2,1)S(1)} %all-reduce.1), kind=kOutput, calls=%fused_computation.2 | convolution fusion | flops 544210944 | bytes 7340032 | tf_op jit(solution)/shard_map/dot_general | solution.py:43
  (2 shorter events, 0.0 us)
Async XLA Ops:
  0.0 205.0 %copy-start = (bf16[256,1024]{1,0:T(8,128)(2,1)S(1)}, bf16[256,1024]{1,0:T(8,128)(2,1)}, u32[]{:S(2)}) copy-start(bf16[256,1024]{1,0:T(8,128)(2,1)} %param.7) | copy-start | bytes 1572868
  0.0 5.0 %copy-start.1 = (bf16[1024,1024]{1,0:T(8,128)(2,1)S(1)}, bf16[1024,1024]{1,0:T(8,128)(2,1)}, u32[]{:S(2)}) copy-start(bf16[1024,1024]{1,0:T(8,128)(2,1)} %param.4) | copy-start | bytes 6291460
  0.0 5.0 %copy-start.2 = (bf16[1024,256]{1,0:T(8,128)(2,1)S(1)}, bf16[1024,256]{1,0:T(8,128)(2,1)}, u32[]{:S(2)}) copy-start(bf16[1024,256]{1,0:T(8,128)(2,1)} %param.6) | copy-start | bytes 1572868
  1.9 27.1 %collective-permute-start = (bf16[512,1024]{1,0:T(8,128)(2,1)S(1)}, bf16[512,1024]{1,0:T(8,128)(2,1)S(1)}, u32[]{:S(2)}, u32[]{:S(2)}) collective-permute-start(bf16[512,1024]{1,0:T(8,128)(2,1)S(1)} %get-tuple-element.7), channel_id=1, source_target_pairs={{0,4},{4,0},{8,12},{12,8},{16,20},{20,16},{24,28},{28,24},{1,5},{5... | collective-permute-start | bytes 3145736 | tf_op jit(solution)/shard_map/ppermute | solution.py:14
  4.9 45.6 %collective-permute-start.1 = (bf16[512,1024]{1,0:T(8,128)(2,1)S(1)}, bf16[512,1024]{1,0:T(8,128)(2,1)S(1)}, u32[]{:S(2)}, u32[]{:S(2)}) collective-permute-start(bf16[512,1024]{1,0:T(8,128)(2,1)S(1)} %get-tuple-element.8), channel_id=1, source_target_pairs={{0,4},{4,0},{8,12},{12,8},{16,20},{20,16},{24,28},{28,24},{1,5},{5... | collective-permute-start | bytes 3145736 | tf_op jit(solution)/shard_map/ppermute | solution.py:14
  5.0 4.7 %slice-start = ((s8[8388608]{0:T(1024)(128)(4,1)}), s8[4194304]{0:T(1024)(128)(4,1)S(1)}, s32[]{:S(2)}) async-start(s8[8388608]{0:T(1024)(128)(4,1)} %bitcast.36), calls=%async_computation | async-start | bytes 8388608
  6.7 3.0 %slice-start.1 = ((s8[8388608]{0:T(1024)(128)(4,1)}), s8[4194304]{0:T(1024)(128)(4,1)S(1)}, s32[]{:S(2)}) async-start(s8[8388608]{0:T(1024)(128)(4,1)} %bitcast.36), calls=%async_computation.1 | async-start | bytes 8388608
  54.5 137.1 %collective-permute-start.2 = (bf16[512,1024]{1,0:T(8,128)(2,1)}, bf16[512,1024]{1,0:T(8,128)(2,1)}, u32[]{:S(2)}, u32[]{:S(2)}) collective-permute-start(bf16[512,1024]{1,0:T(8,128)(2,1)} %get-tuple-element.5), channel_id=1, source_target_pairs={{0,16},{16,0},{4,20},{20,4},{8,24},{24,8},{12,28},{28,12},{1,17},{... | collective-permute-start | bytes 3145736 | tf_op jit(solution)/shard_map/ppermute | solution.py:14
  167.6 36.2 %collective-permute-start.3 = (bf16[512,1024]{1,0:T(8,128)(2,1)}, bf16[512,1024]{1,0:T(8,128)(2,1)S(1)}, u32[]{:S(2)}, u32[]{:S(2)}) collective-permute-start(bf16[512,1024]{1,0:T(8,128)(2,1)} %get-tuple-element.6), channel_id=1, source_target_pairs={{0,16},{16,0},{4,20},{20,4},{8,24},{24,8},{12,28},{28,12},{1,17},{... | collective-permute-start | bytes 3145736 | tf_op jit(solution)/shard_map/ppermute | solution.py:14
  185.6 6.0 %slice-start.2 = ((s8[8388608]{0:T(1024)(128)(4,1)}), s8[4194304]{0:T(1024)(128)(4,1)S(1)}, s32[]{:S(2)}) async-start(s8[8388608]{0:T(1024)(128)(4,1)} %bitcast.38), calls=%async_computation.2 | async-start | bytes 8388608
  188.6 3.0 %slice-start.3 = ((s8[8388608]{0:T(1024)(128)(4,1)}), s8[4194304]{0:T(1024)(128)(4,1)S(1)}, s32[]{:S(2)}) async-start(s8[8388608]{0:T(1024)(128)(4,1)} %bitcast.38), calls=%async_computation.3 | async-start | bytes 8388608
where the time goes:
time: 208 us
  blocking collectives  110 us (53%)
  waiting for transfers between devices  47.8 us (23%)
  starting transfers between devices  24 us (12%)
  matrix products  20.9 us (10%)
  local copies, waits for them, and re-layouts  3.41 us (2%)
    psum x1, blocking collectives, on_device(): rank_total = lax.psum(partial_value, 'feat')  110 us
    ppermute x4, waiting for transfers between devices, swapped(): return lax.ppermute(block, axis, route)  47.8 us
    ppermute x4, starting transfers between devices, swapped(): return lax.ppermute(block, axis, route)  24 us
    dot_general x4, matrix products, pair_product(): jnp.dot(own_rows, section_weight[:block_width], preferred_element_type=jn...  10.2 us
    dot_general x4, matrix products, pair_product(): jnp.dot(partner_rows, section_weight[block_width:], preferred_element_typ...  6.32 us
  transfers between devices with their start and end apart: 4, of which 3 were waited for; matrix products, arithmetic and copies ran while one was open for 8% of the time, Pallas kernels for 0%

commit v1 on v0

v1 whole, which is shorter than its diff:
```python
import functools

import jax
import jax.numpy as jnp
from jax import lax
from jax.experimental import pallas as pl
from jax.experimental.pallas import tpu as pltpu
from jax.sharding import PartitionSpec as P

CHUNKS = 8
MESH = pl.DeviceIdType.MESH


def silu(v):
    return v / (1.0 + jnp.exp(-v))


def flip(me, bits):
    other = me
    for b in bits:
        other = other + (1 - 2 * ((me // (1 << b)) % 2)) * (1 << b)
    return other


def kernel(
    levels, x_hbm, w_hbm, down_hbm, up_hbm, out_hbm,
    x, w0, w1, down, up, xp, state, sp, out,
    acc, low, send_buf, recv_buf, end_recv, mid_recv, end_send, mid_send,
    load_sem, out_sem, ys, yr, zs, zr, rs_s, rs_r, ag_s, ag_r,
    end_s, end_r, mid_s, mid_r, back_s, back_r,
):
    me = lax.axis_index("feat")
    tok, width = x.shape
    rows = tok // CHUNKS
    top = levels - 1
    inner = top - 1

    loads = [
        pltpu.make_async_copy(src, dst, load_sem.at[i])
        for i, (src, dst) in enumerate(
            ((x_hbm, x), (down_hbm, down), (w_hbm.at[0], w0), (w_hbm.at[1], w1), (up_hbm, up))
        )
    ]
    for load in loads:
        load.start()

    partners = [flip(me, (b,)) for b in range(levels)] + [flip(me, (inner, top))]
    barrier = pltpu.get_barrier_semaphore()
    for other in partners:
        pl.semaphore_signal(barrier, inc=1, device_id={"feat": other}, device_id_type=MESH)
    pl.semaphore_wait(barrier, len(partners))

    def remote(src, dst, send, recv, other):
        return pltpu.make_async_remote_copy(
            src_ref=src, dst_ref=dst, send_sem=send, recv_sem=recv,
            device_id={"feat": other}, device_id_type=MESH,
        )

    def part(c):
        return pl.ds(pl.multiple_of(c * rows, rows), rows)

    def y_copy(c):
        return remote(x_hbm.at[part(c)], xp.at[part(c)], ys.at[c], yr.at[c], partners[0])

    def z_copy(c):
        return remote(state.at[part(c)], sp.at[part(c)], zs.at[c], zr.at[c], partners[top])

    def out_copy(c):
        return pltpu.make_async_copy(out.at[part(c)], out_hbm.at[part(c)], out_sem.at[c])

    y_copy(0).start()

    loads[0].wait()
    loads[1].wait()
    bit = [(me // (1 << b)) % 2 for b in range(levels)]
    step_rows = tok // 8

    def project(offset, count):
        @pl.loop(0, count // step_rows)
        def _(i):
            span = pl.ds(pl.multiple_of(offset + i * step_rows, step_rows), step_rows)
            acc[span, :] = jnp.dot(x[span, :], down[...], preferred_element_type=jnp.float32)

    def span_of(offset, count):
        return pl.ds(pl.multiple_of(offset, count), count)

    half = tok // 2
    keep = bit[0] * half
    away = (1 - bit[0]) * half
    project(away, half)
    spans = [(keep, away, half)]
    for b in range(1, inner):
        size = spans[-1][2] // 2
        base = spans[-1][0]
        spans.append((base + bit[b] * size, base + (1 - bit[b]) * size, size))

    def rs_copy(b):
        size = spans[b][2]
        start = tok - 2 * size
        return remote(
            send_buf.at[pl.ds(start, size)], recv_buf.at[pl.ds(start, size)],
            rs_s.at[b], rs_r.at[b], partners[b],
        )

    def rs_start(b):
        _, gone, size = spans[b]
        send_buf[pl.ds(tok - 2 * size, size), :] = acc[span_of(gone, size), :].astype(jnp.bfloat16)
        rs_copy(b).start()

    def rs_finish(b):
        kept, _, size = spans[b]
        rs_copy(b).wait_recv()
        acc[span_of(kept, size), :] += recv_buf[pl.ds(tok - 2 * size, size), :].astype(jnp.float32)

    rs_start(0)
    for c in range(1, CHUNKS):
        y_copy(c).start()
    project(keep, half)

    own, _, own_size = spans[-1]
    own_span = span_of(own, own_size)
    middle = (bit[inner] + bit[top]) % 2
    end_copy = remote(end_send, end_recv, end_s.at[0], end_r.at[0], partners[inner])
    mid_copy = remote(mid_send, mid_recv, mid_s.at[0], mid_r.at[0], partners[levels])
    back_copy = remote(low.at[own_span], low.at[own_span], back_s.at[0], back_r.at[0], partners[inner])

    def to_middle():
        @pl.when(middle == 0)
        def _():
            end_send[...] = acc[own_span, :].astype(jnp.bfloat16)
            end_copy.start()

    def across():
        @pl.when(middle == 1)
        def _():
            end_copy.wait_recv()
            acc[own_span, :] += end_recv[...].astype(jnp.float32)
            mid_send[...] = acc[own_span, :].astype(jnp.bfloat16)
            mid_copy.start()

    def back():
        @pl.when(middle == 1)
        def _():
            mid_copy.wait_recv()
            low[own_span, :] = (acc[own_span, :] + mid_recv[...].astype(jnp.float32)).astype(jnp.bfloat16)
            back_copy.start()

    def ag_copy(b):
        size = tok >> (b + 1)
        span = span_of(spans[b][0], size)
        return remote(low.at[span], low.at[span], ag_s.at[b], ag_r.at[b], partners[b])

    columns = 512
    column_tiles = width // columns

    def first_section(c):
        y_copy(c).wait_recv()

        @pl.loop(0, column_tiles)
        def _(t):
            cols = pl.ds(pl.multiple_of(t * columns, columns), columns)
            pre = jnp.dot(x[part(c), :], w0[:width, cols], preferred_element_type=jnp.float32)
            pre += jnp.dot(xp[part(c), :], w0[width:, cols], preferred_element_type=jnp.float32)
            state[part(c), cols] = silu(pre).astype(jnp.bfloat16)

        z_copy(c).start()

    def second_section(c):
        z_copy(c).wait_recv()

        @pl.loop(0, column_tiles)
        def _(t):
            cols = pl.ds(pl.multiple_of(t * columns, columns), columns)
            pre = jnp.dot(state[part(c), :], w1[:width, cols], preferred_element_type=jnp.float32)
            pre += jnp.dot(sp[part(c), :], w1[width:, cols], preferred_element_type=jnp.float32)
            side = jnp.dot(low[part(c), :], up[:, cols], preferred_element_type=jnp.float32)
            out[part(c), cols] = (silu(pre) + side).astype(jnp.bfloat16)

        out_copy(c).start()

    loads[2].wait()
    first_section(0)
    for b in range(inner):
        rs_finish(b)
        if b + 1 < inner:
            rs_start(b + 1)
    to_middle()

    @pl.loop(1, 3)
    def _(c):
        first_section(c)

    across()

    @pl.loop(3, CHUNKS)
    def _(c):
        first_section(c)

    back()

    @pl.when(middle == 0)
    def _():
        back_copy.wait_recv()

    for b in range(inner - 1, -1, -1):
        ag_copy(b).start()
        ag_copy(b).wait_recv()

    loads[3].wait()
    loads[4].wait()

    @pl.loop(0, CHUNKS)
    def _(c):
        second_section(c)

    @pl.loop(0, CHUNKS)
    def _(c):
        y_copy(c).wait_send()
        z_copy(c).wait_send()
        out_copy(c).wait()

    for b in range(inner):
        rs_copy(b).wait_send()
        ag_copy(b).wait_send()

    @pl.when(middle == 0)
    def _():
        end_copy.wait_send()

    @pl.when(middle == 1)
    def _():
        mid_copy.wait_send()
        back_copy.wait_send()


def on_device(tokens, pair_weights, rank_down, rank_up):
    levels = lax.axis_size("feat").bit_length() - 1
    inner = levels - 2
    tok, width = tokens.shape
    rank = rank_down.shape[1]
    own = tok >> inner
    bf16 = jnp.bfloat16
    dma = pltpu.SemaphoreType.DMA
    any_spec = pl.BlockSpec(memory_space=pl.ANY)
    return pl.pallas_call(
        functools.partial(kernel, levels),
        out_shape=jax.ShapeDtypeStruct((tok, width), bf16),
        in_specs=[any_spec] * 4,
        out_specs=any_spec,
        scratch_shapes=[
            pltpu.VMEM((tok, width), bf16),
            pltpu.VMEM(pair_weights.shape[1:], bf16),
            pltpu.VMEM(pair_weights.shape[1:], bf16),
            pltpu.VMEM((width, rank), bf16),
            pltpu.VMEM((rank, width), bf16),
            pltpu.VMEM((tok, width), bf16),
            pltpu.VMEM((tok, width), bf16),
            pltpu.VMEM((tok, width), bf16),
            pltpu.VMEM((tok, width), bf16),
            pltpu.VMEM((tok, rank), jnp.float32),
            pltpu.VMEM((tok, rank), bf16),
            pltpu.VMEM((tok, rank), bf16),
            pltpu.VMEM((tok, rank), bf16),
            pltpu.VMEM((own, rank), bf16),
            pltpu.VMEM((own, rank), bf16),
            pltpu.VMEM((own, rank), bf16),
            pltpu.VMEM((own, rank), bf16),
            dma((5,)), dma((CHUNKS,)),
            dma((CHUNKS,)), dma((CHUNKS,)), dma((CHUNKS,)), dma((CHUNKS,)),
            dma((inner,)), dma((inner,)), dma((inner,)), dma((inner,)),
            dma((1,)), dma((1,)), dma((1,)), dma((1,)), dma((1,)), dma((1,)),
        ],
        compiler_params=pltpu.CompilerParams(
            collective_id=0, has_side_effects=True, vmem_limit_bytes=60 * 2**20
        ),
    )(tokens, pair_weights, rank_down, rank_up)


def solution(mesh):
    return jax.shard_map(
        on_device,
        mesh=mesh,
        in_specs=(P("tok", "feat"), P(None, None, "feat"), P("feat", None), P(None, "feat")),
        out_specs=P("tok", "feat"),
        check_vma=False,
    )
```

time: 208 us -> 134 us (0.64)
  Pallas kernels: 0 us -> 131 us
  blocking collectives: 110 us -> 0 us
  waiting for transfers between devices: 47.8 us -> 0 us
  starting transfers between devices: 24 us -> 0 us
  matrix products: 20.9 us -> 0 us
    pallas_call x0 -> x1, Pallas kernels: none -> 131 us  [on_device(): pl.pallas_call(functools.partial(kernel, levels), out_shape=jax.ShapeDtyp...]
    psum x1 -> x0, blocking collectives: 110 us -> none  [on_device(): rank_total = lax.psum(partial_value, 'feat')]
    ppermute x4 -> x0, waiting for transfers between devices: 47.8 us -> none  [swapped(): return lax.ppermute(block, axis, route)]
    ppermute x4 -> x0, starting transfers between devices: 24 us -> none  [swapped(): return lax.ppermute(block, axis, route)]
    dot_general x10 -> x0, matrix products: 20.9 us -> none  [the longest x4 10.2 us: pair_product(): jnp.dot(own_rows, section_weight[:block_width], preferred_element_type=jn...]
    slice x2 -> x0, local copies, waits for them, and re-layouts: 3.36 us -> none  [on_device(): own_rows = current[half_index * half_rows:(half_index + 1) * half_rows]]
    unnamed x14 -> x1, local copies, waits for them, and re-layouts: 0.05 us -> 3.08 us
  transfers between devices with their start and end apart: 4 -> 0, of which waited for: 3 -> 0; matrix products, arithmetic and copies ran while one was open for 8% -> 0% of each run, Pallas kernels for 0% -> 0%
where the time goes in v1:
time: 134 us
  Pallas kernels  131 us (98%)
  local copies, waits for them, and re-layouts  3.08 us (2%)
    pallas_call x1, Pallas kernels, on_device(): pl.pallas_call(functools.partial(kernel, levels), out_shape=jax.ShapeDtyp...  131 us
    unnamed x1, local copies, waits for them, and re-layouts  3.08 us

profile of v1, /device:TPU:0, one launch (start us, length us, event | category | flops | bytes accessed | tf_op | source)
XLA Modules:
  0.0 134.2 jit_solution(15183712227834772183)
XLA Ops:
  0.0 131.1 %shard_map.46 = bf16[1024,1024]{1,0:T(8,128)(2,1)} custom-call(bf16[1024,1024]{1,0:T(8,128)(2,1)} %x_hbm.1, bf16[2,2048,1024]{2,1,0:T(8,128)(2,1)} %w_hbm.1, bf16[1024,256]{1,0:T(8,128)(2,1)} %down_hbm.1, bf16[256,1024]{1,0:T(8,128)(2,1)} %up_hbm.1), custom_call_target="tpu_custom_call" | custom-call | tf_op jit(solution)/shard_map/pallas_call | solution.py:245
  131.1 3.1 %copy.6 = bf16[1024,1024]{1,0:T(8,128)(2,1)} copy(bf16[1024,1024]{1,0:T(8,128)(2,1)} %shard_map.46) | data formatting | bytes 4194304

commit v2 on v1

--- a/solution.py
+++ b/solution.py
@@ -7,7 +7,7 @@
 from jax.experimental.pallas import tpu as pltpu
 from jax.sharding import PartitionSpec as P
 
-CHUNKS = 8
+CHUNKS = 16
 MESH = pl.DeviceIdType.MESH
 
 
@@ -178,29 +178,29 @@
 
         out_copy(c).start()
 
+    def sections(first, last):
+        @pl.loop(first, last)
+        def _(c):
+            first_section(c)
+
     loads[2].wait()
-    first_section(0)
+    sections(0, 1)
     for b in range(inner):
         rs_finish(b)
         if b + 1 < inner:
             rs_start(b + 1)
     to_middle()
-
-    @pl.loop(1, 3)
-    def _(c):
-        first_section(c)
-
+    sections(1, 2)
     across()
-
-    @pl.loop(3, CHUNKS)
-    def _(c):
-        first_section(c)
-
+    hold = 4 + middle * (6 - 4)
+    sections(2, hold)
     back()
 
     @pl.when(middle == 0)
     def _():
         back_copy.wait_recv()
+
+    sections(hold, CHUNKS)
 
     for b in range(inner - 1, -1, -1):
         ag_copy(b).start()

time: 134 us -> 121 us (0.903)
  Pallas kernels: 131 us -> 118 us
    pallas_call x1, Pallas kernels: 131 us -> 118 us  [on_device(): pl.pallas_call(functools.partial(kernel, levels), out_shape=jax.ShapeDtyp...]
where the time goes in v2:
time: 121 us
  Pallas kernels  118 us (98%)
  local copies, waits for them, and re-layouts  3.08 us (3%)
    pallas_call x1, Pallas kernels, on_device(): pl.pallas_call(functools.partial(kernel, levels), out_shape=jax.ShapeDtyp...  118 us
    unnamed x1, local copies, waits for them, and re-layouts  3.08 us

profile of v2, /device:TPU:0, one launch (start us, length us, event | category | flops | bytes accessed | tf_op | source)
XLA Modules:
  0.0 120.8 jit_solution(13320784112689859191)
XLA Ops:
  0.0 117.7 %shard_map.46 = bf16[1024,1024]{1,0:T(8,128)(2,1)} custom-call(bf16[1024,1024]{1,0:T(8,128)(2,1)} %x_hbm.1, bf16[2,2048,1024]{2,1,0:T(8,128)(2,1)} %w_hbm.1, bf16[1024,256]{1,0:T(8,128)(2,1)} %down_hbm.1, bf16[256,1024]{1,0:T(8,128)(2,1)} %up_hbm.1), custom_call_target="tpu_custom_call" | custom-call | tf_op jit(solution)/shard_map/pallas_call | solution.py:245
  117.7 3.1 %copy.6 = bf16[1024,1024]{1,0:T(8,128)(2,1)} copy(bf16[1024,1024]{1,0:T(8,128)(2,1)} %shard_map.46) | data formatting | bytes 4194304

commit v3 on v2

--- a/solution.py
+++ b/solution.py
@@ -41,7 +41,7 @@
             ((x_hbm, x), (down_hbm, down), (w_hbm.at[0], w0), (w_hbm.at[1], w1), (up_hbm, up))
         )
     ]
-    for load in loads:
+    for load in loads[:3]:
         load.start()
 
     partners = [flip(me, (b,)) for b in range(levels)] + [flip(me, (inner, top))]
@@ -115,7 +115,8 @@
     rs_start(0)
     for c in range(1, CHUNKS):
         y_copy(c).start()
-    project(keep, half)
+    for load in loads[3:]:
+        load.start()
 
     own, _, own_size = spans[-1]
     own_span = span_of(own, own_size)
@@ -150,7 +151,7 @@
         span = span_of(spans[b][0], size)
         return remote(low.at[span], low.at[span], ag_s.at[b], ag_r.at[b], partners[b])
 
-    columns = 512
+    columns = width
     column_tiles = width // columns
 
     def first_section(c):
@@ -185,6 +186,7 @@
 
     loads[2].wait()
     sections(0, 1)
+    project(keep, half)
     for b in range(inner):
         rs_finish(b)
         if b + 1 < inner:

time: 121 us -> 120 us (level)
  Pallas kernels: 118 us -> 116 us
    pallas_call x1, Pallas kernels: 118 us -> 116 us  [on_device(): pl.pallas_call(functools.partial(kernel, levels), out_shape=jax.ShapeDtyp...]
where the time goes in v3:
time: 120 us; the launch traced here: 119 us
  Pallas kernels  116 us (97%)
  local copies, waits for them, and re-layouts  3.08 us (3%)
    pallas_call x1, Pallas kernels, on_device(): pl.pallas_call(functools.partial(kernel, levels), out_shape=jax.ShapeDtyp...  116 us
    unnamed x1, local copies, waits for them, and re-layouts  3.08 us

profile of v3, /device:TPU:0, one launch (start us, length us, event | category | flops | bytes accessed | tf_op | source)
XLA Modules:
  0.0 118.8 jit_solution(14828485549605460402)
XLA Ops:
  0.0 115.7 %shard_map.46 = bf16[1024,1024]{1,0:T(8,128)(2,1)} custom-call(bf16[1024,1024]{1,0:T(8,128)(2,1)} %x_hbm.1, bf16[2,2048,1024]{2,1,0:T(8,128)(2,1)} %w_hbm.1, bf16[1024,256]{1,0:T(8,128)(2,1)} %down_hbm.1, bf16[256,1024]{1,0:T(8,128)(2,1)} %up_hbm.1), custom_call_target="tpu_custom_call" | custom-call | tf_op jit(solution)/shard_map/pallas_call | solution.py:247
  115.7 3.1 %copy.6 = bf16[1024,1024]{1,0:T(8,128)(2,1)} copy(bf16[1024,1024]{1,0:T(8,128)(2,1)} %shard_map.46) | data formatting | bytes 4194304
